TPU v7x, 512 devices: a whole 4x4x16 slice. The times are simulated.
512 devices in a mesh: db: 16 (over y_hi, x, core), pb: 32 (over y_lo, z).
Axes of the slice: x: 4, y: 4 (y_hi: 2, y_lo: 2; y = y_hi * 2 + y_lo), z: 16, core: 2. Of those that a mesh axis runs over, the one named last changes fastest.
Arguments:
- queries: bfloat16 [8192, 768], P(('db', 'pb')), may hold values from -14 to 14
- passage_codes: int32 [65536, 64], P(('db', 'pb')), may hold values from 0 to 255
- codebooks: bfloat16 [64, 12, 256], replicated, may hold values from -4 to 4
- positives: int32 [8192], P(('db', 'pb')), may hold values from 0 to 2047
- loss_weight: float32 [8192], P(('db', 'pb')), may hold values from -12 to 12
Outputs:
- query_loss: float32 [8192], P(('db', 'pb'))
- grad_queries: float32 [8192, 768], P(('db', 'pb'))
- grad_codebooks: float32 [64, 12, 256], replicated
All inputs are finite; a program needn't handle non-finite values.
Results may differ from a plain program's by a relative error of at most 0.0055.
Values may be sent and summed in bfloat16 or wider, within the bound.
No kernel may reach another device: no remote copies, remote signals or barrier semaphores. Data moves between devices by JAX's collectives and lax.ppermute only.
A program may use at most 64 MiB of HBM per device.

v0:
```python
import math
import jax
import jax.numpy as jnp
from jax import lax
from jax.sharding import PartitionSpec as P


def shifted(block, axis, distance):
    devices = range(lax.axis_size(axis))
    route = [((i - distance) % len(devices), i) for i in devices]
    return lax.ppermute(block, axis, route)


def code_table(code_rows, level_count):
    levels = jnp.arange(level_count, dtype=jnp.int32)
    return (levels[None, :, None] == code_rows[:, None, :]).astype(jnp.bfloat16)


def decode_cols(codebooks, passage_codes):
    book_count, sub_width, level_count = codebooks.shape
    passage_count = passage_codes.shape[0]
    code_sets = passage_codes.T.reshape(book_count // 4, 4, passage_count)
    book_sets = codebooks.reshape(book_count // 4, 4, sub_width, level_count)

    def decode_book_set(set_items):
        code_rows, book_rows = set_items
        table = code_table(code_rows, level_count)
        return jnp.einsum("mck,mkp->mcp", book_rows, table, preferred_element_type=jnp.float32)

    picked = lax.map(decode_book_set, (code_sets, book_sets))
    return picked.reshape(book_count * sub_width, passage_count).astype(jnp.bfloat16)


def book_part(passage_codes, grad_cols, codebooks):
    book_count, sub_width, level_count = codebooks.shape
    passage_count = passage_codes.shape[0]
    code_sets = passage_codes.T.reshape(book_count // 4, 4, passage_count)
    grad_sets = grad_cols.reshape(book_count // 4, 4, sub_width, passage_count)

    def book_book_set(set_items):
        code_rows, grad_rows = set_items
        table = code_table(code_rows, level_count)
        high_part = grad_rows.astype(jnp.bfloat16)
        low_part = (grad_rows - high_part.astype(jnp.float32)).astype(jnp.bfloat16)
        high_sum = jnp.einsum("mcp,mkp->mck", high_part, table, preferred_element_type=jnp.float32)
        low_sum = jnp.einsum("mcp,mkp->mck", low_part, table, preferred_element_type=jnp.float32)
        return high_sum + low_sum

    return lax.map(book_book_set, (code_sets, grad_sets)).reshape(
        book_count, sub_width, level_count
    )


def move_block(query_block):
    moved_block = shifted(query_block, "db", 1)
    return moved_block


def move_stats(running_max, running_sum):
    moved_stats = shifted((running_max, running_sum), "db", 1)
    return moved_stats


def move_grads(log_total, block_weight, block_target, block_chosen, block_grad):
    moved_grads = shifted(
        (log_total, block_weight, block_target, block_chosen, block_grad), "db", 1
    )
    return moved_grads


def fold_stats(running, scores):
    running_max, running_sum = running
    newest_max = jnp.maximum(running_max, jnp.max(scores, axis=1))
    running_sum = running_sum * jnp.exp(running_max - newest_max) + jnp.sum(
        jnp.exp(scores - newest_max[:, None]), axis=1
    )
    return (newest_max, running_sum)


def per_device(queries, passage_codes, codebooks, positives, loss_weight):
    query_rows, model_width = queries.shape
    passage_count = passage_codes.shape[0]
    logit_scale = 2.5 / math.sqrt(model_width)
    empty_max = jnp.full((query_rows,), -jnp.inf, jnp.float32)
    empty_rows = jnp.zeros((query_rows,), jnp.float32)
    empty_grad = jnp.zeros((query_rows, model_width), jnp.float32)
    decoded_cols = decode_cols(codebooks, passage_codes)
    spot_index = (
        lax.axis_index("db") * passage_count + jnp.arange(passage_count, dtype=jnp.int32)
    ).astype(jnp.float32)

    def stats_step(turn_index, state):
        query_block, running_max, running_sum = state
        scores = (
            jnp.dot(query_block, decoded_cols, preferred_element_type=jnp.float32) * logit_scale
        )
        newest_max, running_sum = fold_stats((running_max, running_sum), scores)
        query_block = move_block(query_block)
        newest_max, running_sum = move_stats(newest_max, running_sum)
        return (query_block, newest_max, running_sum)

    query_block, running_max, running_sum = lax.fori_loop(
        0, lax.axis_size("db"), stats_step, (queries, empty_max, empty_rows)
    )
    log_total = running_max + jnp.log(running_sum)

    def grad_step(turn_index, state):
        (
            query_block,
            block_total,
            block_weight,
            block_target,
            block_chosen,
            block_grad,
            passage_grad,
        ) = state
        scores = (
            jnp.dot(query_block, decoded_cols, preferred_element_type=jnp.float32) * logit_scale
        )
        is_positive = block_target[:, None] == spot_index[None, :]
        block_chosen = block_chosen + jnp.sum(jnp.where(is_positive, scores, 0.0), axis=1)
        coefficient = (
            block_weight[:, None]
            * (jnp.exp(scores - block_total[:, None]) - is_positive.astype(jnp.float32))
            * logit_scale
        ).astype(jnp.bfloat16)
        block_grad = block_grad + jnp.einsum(
            "qp,dp->qd", coefficient, decoded_cols, preferred_element_type=jnp.float32
        )
        passage_grad = passage_grad + jnp.einsum(
            "qd,qp->dp", query_block, coefficient, preferred_element_type=jnp.float32
        )
        query_block = move_block(query_block)
        block_total, block_weight, block_target, block_chosen, block_grad = move_grads(
            block_total, block_weight, block_target, block_chosen, block_grad
        )
        return (
            query_block,
            block_total,
            block_weight,
            block_target,
            block_chosen,
            block_grad,
            passage_grad,
        )

    start_state = (
        queries,
        log_total,
        loss_weight,
        positives.astype(jnp.float32),
        empty_rows,
        empty_grad,
        jnp.zeros((model_width, passage_count), jnp.float32),
    )
    final_state = lax.fori_loop(0, lax.axis_size("db"), grad_step, start_state)
    chosen = final_state[4]
    grad_queries = final_state[5]
    book_grad = book_part(passage_codes, final_state[6], codebooks)
    query_loss = loss_weight * (log_total - chosen)
    book_total = lax.psum(book_grad, ("db", "pb"))
    return (query_loss, grad_queries, book_total)


def solution(mesh):
    return jax.shard_map(
        per_device,
        mesh=mesh,
        in_specs=(
            P(("db", "pb"), None),
            P(("db", "pb"), None),
            P(),
            P(("db", "pb")),
            P(("db", "pb")),
        ),
        out_specs=(P(("db", "pb")), P(("db", "pb"), None), P()),
        check_vma=False,
    )
```

profile of v0, /device:TPU:2, one launch (start us, length us, event | category | flops | bytes accessed | tf_op | source)
XLA Modules:
  0.0 1143.5 jit_solution(6119165569938202182)
XLA Ops:
  9.2 14.4 %while.57 = (s32[]{:T(128)}, bf16[16,4,12,128]{3,2,1,0:T(8,128)(2,1)S(1)}, bf16[16,4,12,256]{3,2,1,0:T(8,128)(2,1)S(1)}, s32[16,4,128]{2,1,0:T(4,128)}, s32[]{:T(128)}) while((s32[]{:T(128)}, bf16[16,4,12,128]{3,2,1,0:T(8,128)(2,1)S(1)}, bf16[16,4,12,256]{3,2,1,0:T(8,128)(2,1)S(1)}, s32[16,4,128]{2,1,0:T(4,128)}, s32[]{:T(128)}) %tuple.90), condition=%wide.region_1.2_spmd, body=%wide.region_0.1_spmd.sunk | while | flops 3276802 | bytes 72769 | solution.py:30
  23.6 202.0 %while.58 = (s32[]{:T(128)}, bf16[16,768]{1,0:T(8,128)(2,1)S(1)}, f32[16]{0:T(128)S(1)}, f32[16]{0:T(128)S(1)}, bf16[768,128]{1,0:T(8,128)(2,1)S(1)}, /*index=5*/s32[]{:T(128)}) while((s32[]{:T(128)}, bf16[16,768]{1,0:T(8,128)(2,1)S(1)}, f32[16]{0:T(128)S(1)}, f32[16]{0:T(128)S(1)}, bf16[768,128]{1,0:T(8,128)(2,1)S(1)}, ...), condition=%wide.region_5.6_spmd, body=%wide.region_2.5_spmd.sunk | while | flops 3153954 | bytes 386557 | solution.py:102
  48.1 4.2 collective-permute-start.1
  52.4 4.9 collective-permute-start.2
  62.5 4.2 collective-permute-start.1
  75.3 4.2 collective-permute-start.1
  88.1 4.2 collective-permute-start.1
  100.9 4.2 collective-permute-start.1
  113.7 4.2 collective-permute-start.1
  126.6 4.2 collective-permute-start.1
  139.4 4.2 collective-permute-start.1
  152.2 4.2 collective-permute-start.1
  165.0 4.2 collective-permute-start.1
  177.9 4.2 collective-permute-start.1
  190.7 4.2 collective-permute-start.1
  203.5 4.2 collective-permute-start.1
  216.3 4.2 collective-permute-start.1
  227.5 404.8 %while.60 = (s32[]{:T(128)}, bf16[16,768]{1,0:T(8,128)(2,1)S(1)}, f32[16]{0:T(128)S(1)}, f32[16]{0:T(128)S(1)}, f32[16]{0:T(128)S(1)}, /*index=5*/f32[16]{0:T(12...) while((s32[]{:T(128)}, bf16[16,768]{1,0:T(8,128)(2,1)S(1)}, ...), condition=%wide.region_8.9_spmd.clone, body=%wide.region_6.8_spmd.clone.sunk | while | flops 9683203 | bytes 1700275 | solution.py:156
  230.7 4.2 collective-permute-start.3
  238.7 4.2 collective-permute-start.8
  256.0 4.2 collective-permute-start.3
  264.6 4.6 collective-permute-start.7
  270.0 7.7 collective-permute-start.5
  278.5 4.1 collective-permute-start.6
  282.6 4.2 collective-permute-start.3
  296.1 6.9 collective-permute-start.5
  303.8 4.1 collective-permute-start.6
  307.9 4.2 collective-permute-start.3
  321.3 6.9 collective-permute-start.5
  329.0 4.1 collective-permute-start.6
  333.1 4.2 collective-permute-start.3
  346.6 6.9 collective-permute-start.5
  354.3 4.1 collective-permute-start.6
  358.4 4.2 collective-permute-start.3
  371.9 6.9 collective-permute-start.5
  379.6 4.1 collective-permute-start.6
  383.7 4.2 collective-permute-start.3
  397.1 6.9 collective-permute-start.5
  404.8 4.1 collective-permute-start.6
  408.9 4.2 collective-permute-start.3
  422.4 6.9 collective-permute-start.5
  430.1 4.1 collective-permute-start.6
  434.2 4.2 collective-permute-start.3
  447.7 6.9 collective-permute-start.5
  455.4 4.1 collective-permute-start.6
  459.5 4.2 collective-permute-start.3
  472.9 6.9 collective-permute-start.5
  480.6 4.1 collective-permute-start.6
  484.7 4.2 collective-permute-start.3
  498.2 6.9 collective-permute-start.5
  510.0 4.2 collective-permute-start.3
  523.5 6.9 collective-permute-start.5
  535.3 4.2 collective-permute-start.3
  548.8 6.9 collective-permute-start.5
  556.4 4.1 collective-permute-start.6
  560.5 4.2 collective-permute-start.3
  574.0 6.9 collective-permute-start.5
  581.7 4.1 collective-permute-start.6
  585.8 4.2 collective-permute-start.3
  599.3 6.9 collective-permute-start.5
  611.1 4.2 collective-permute-start.3
  624.6 6.9 collective-permute-start.5
  632.5 17.6 %while.59 = (s32[]{:T(128)}, f32[16,4,12,256]{3,2,1,0:T(8,128)S(1)}, f32[16,4,12,128]{3,2,1,0:T(8,128)S(1)}, s32[16,4,128]{2,1,0:T(4,128)}, s32[]{:T(128)}) while((s32[]{:T(128)}, f32[16,4,12,256]{3,2,1,0:T(8,128)S(1)}, f32[16,4,12,128]{3,2,1,0:T(8,128)S(1)}, s32[16,4,128]{2,1,0:T(4,128)}, s32[]{:T(128)}) %tuple.91), condition=%wide.region_10.11_spmd, body=%wide.region_9.10_spmd.sunk | while | flops 6590466 | bytes 238661 | solution.py:49
  652.6 481.5 %all-reduce.2.cloned.1.call-done = f32[64,12,256]{2,0,1:T(8,128)} async-done(((f32[64,12,256]{2,0,1:T(8,128)}), f32[64,12,256]{2,0,1:T(8,128)}) %all-reduce.2.cloned.1.call-update) | async-done | bytes 786448 | tf_op jit(solution)/shard_map/psum | solution.py:161
  (582 shorter events, 356.9 us)
Async XLA Ops:
  7.2 1126.9 %all-reduce.2.cloned.1.call-start = ((), (), s32[]{:S(2)}) async-start(), calls=%async_computation | async-start | bytes 1572864 | tf_op jit(solution)/shard_map/psum | solution.py:161
  227.5 23.6 %collective-permute-start.6 = (f32[16]{0:T(128)S(1)}, f32[16]{0:T(128)S(1)}, u32[]{:S(2)}, u32[]{:S(2)}) collective-permute-start(f32[16]{0:T(128)S(1)} %copy.47), channel_id=1, source_target_pairs={{480,0},{0,32},{32,64},{64,96},{96,128},{128,160},{160,192},{192,2... | collective-permute-start | bytes 200 | tf_op jit(solution)/shard_map/while/body/eval_jaxpr/ppermute | solution.py:11
  230.7 22.0 %collective-permute-start.3 = (bf16[16,768]{1,0:T(8,128)(2,1)S(1)}, bf16[16,768]{1,0:T(8,128)(2,1)S(1)}, u32[]{:S(2)}, u32[]{:S(2)}) collective-permute-start(bf16[16,768]{1,0:T(8,128)(2,1)S(1)} %copy.44), channel_id=1, source_target_pairs={{480,0},{0,32},{32,64},{64,96},{96,128},{128,160},{160,192},{192,2... | collective-permute-start | bytes 73736 | tf_op jit(solution)/shard_map/while/body/eval_jaxpr/ppermute | solution.py:11
  234.9 16.2 %collective-permute-start.4 = (f32[16]{0:T(128)S(1)}, f32[16]{0:T(128)S(1)}, u32[]{:S(2)}, u32[]{:S(2)}) collective-permute-start(f32[16]{0:T(128)S(1)} %copy.45), channel_id=1, source_target_pairs={{480,0},{0,32},{32,64},{64,96},{96,128},{128,160},{160,192},{192,2... | collective-permute-start | bytes 200 | tf_op jit(solution)/shard_map/while/body/eval_jaxpr/ppermute | solution.py:11
  252.7 25.0 %collective-permute-start.6 = (f32[16]{0:T(128)S(1)}, f32[16]{0:T(128)S(1)}, u32[]{:S(2)}, u32[]{:S(2)}) collective-permute-start(f32[16]{0:T(128)S(1)} %copy.47), channel_id=1, source_target_pairs={{480,0},{0,32},{32,64},{64,96},{96,128},{128,160},{160,192},{192,2... | collective-permute-start | bytes 200 | tf_op jit(solution)/shard_map/while/body/eval_jaxpr/ppermute | solution.py:11
  256.0 22.5 %collective-permute-start.3 = (bf16[16,768]{1,0:T(8,128)(2,1)S(1)}, bf16[16,768]{1,0:T(8,128)(2,1)S(1)}, u32[]{:S(2)}, u32[]{:S(2)}) collective-permute-start(bf16[16,768]{1,0:T(8,128)(2,1)S(1)} %copy.44), channel_id=1, source_target_pairs={{480,0},{0,32},{32,64},{64,96},{96,128},{128,160},{160,192},{192,2... | collective-permute-start | bytes 73736 | tf_op jit(solution)/shard_map/while/body/eval_jaxpr/ppermute | solution.py:11
  260.2 17.5 %collective-permute-start.4 = (f32[16]{0:T(128)S(1)}, f32[16]{0:T(128)S(1)}, u32[]{:S(2)}, u32[]{:S(2)}) collective-permute-start(f32[16]{0:T(128)S(1)} %copy.45), channel_id=1, source_target_pairs={{480,0},{0,32},{32,64},{64,96},{96,128},{128,160},{160,192},{192,2... | collective-permute-start | bytes 200 | tf_op jit(solution)/shard_map/while/body/eval_jaxpr/ppermute | solution.py:11
  262.6 15.9 %collective-permute-start.8 = (f32[16,768]{1,0:T(8,128)S(1)}, f32[16,768]{1,0:T(8,128)S(1)}, u32[]{:S(2)}, u32[]{:S(2)}) collective-permute-start(f32[16,768]{1,0:T(8,128)S(1)} %convolution_add_fusion.3), channel_id=1, source_target_pairs={{480,0},{0,32},{32,64},{64,96},{96,128},{128,160},{160,192},{192,2... | collective-permute-start | bytes 147464 | tf_op jit(solution)/shard_map/while/body/eval_jaxpr/ppermute | solution.py:11
  278.5 24.5 %collective-permute-start.6 = (f32[16]{0:T(128)S(1)}, f32[16]{0:T(128)S(1)}, u32[]{:S(2)}, u32[]{:S(2)}) collective-permute-start(f32[16]{0:T(128)S(1)} %copy.47), channel_id=1, source_target_pairs={{480,0},{0,32},{32,64},{64,96},{96,128},{128,160},{160,192},{192,2... | collective-permute-start | bytes 200 | tf_op jit(solution)/shard_map/while/body/eval_jaxpr/ppermute | solution.py:11
  282.6 21.2 %collective-permute-start.3 = (bf16[16,768]{1,0:T(8,128)(2,1)S(1)}, bf16[16,768]{1,0:T(8,128)(2,1)S(1)}, u32[]{:S(2)}, u32[]{:S(2)}) collective-permute-start(bf16[16,768]{1,0:T(8,128)(2,1)S(1)} %copy.44), channel_id=1, source_target_pairs={{480,0},{0,32},{32,64},{64,96},{96,128},{128,160},{160,192},{192,2... | collective-permute-start | bytes 73736 | tf_op jit(solution)/shard_map/while/body/eval_jaxpr/ppermute | solution.py:11
  286.8 16.2 %collective-permute-start.4 = (f32[16]{0:T(128)S(1)}, f32[16]{0:T(128)S(1)}, u32[]{:S(2)}, u32[]{:S(2)}) collective-permute-start(f32[16]{0:T(128)S(1)} %copy.45), channel_id=1, source_target_pairs={{480,0},{0,32},{32,64},{64,96},{96,128},{128,160},{160,192},{192,2... | collective-permute-start | bytes 200 | tf_op jit(solution)/shard_map/while/body/eval_jaxpr/ppermute | solution.py:11
  289.2 14.5 %collective-permute-start.8 = (f32[16,768]{1,0:T(8,128)S(1)}, f32[16,768]{1,0:T(8,128)S(1)}, u32[]{:S(2)}, u32[]{:S(2)}) collective-permute-start(f32[16,768]{1,0:T(8,128)S(1)} %convolution_add_fusion.3), channel_id=1, source_target_pairs={{480,0},{0,32},{32,64},{64,96},{96,128},{128,160},{160,192},{192,2... | collective-permute-start | bytes 147464 | tf_op jit(solution)/shard_map/while/body/eval_jaxpr/ppermute | solution.py:11
  303.8 24.5 %collective-permute-start.6 = (f32[16]{0:T(128)S(1)}, f32[16]{0:T(128)S(1)}, u32[]{:S(2)}, u32[]{:S(2)}) collective-permute-start(f32[16]{0:T(128)S(1)} %copy.47), channel_id=1, source_target_pairs={{480,0},{0,32},{32,64},{64,96},{96,128},{128,160},{160,192},{192,2... | collective-permute-start | bytes 200 | tf_op jit(solution)/shard_map/while/body/eval_jaxpr/ppermute | solution.py:11
  307.9 21.2 %collective-permute-start.3 = (bf16[16,768]{1,0:T(8,128)(2,1)S(1)}, bf16[16,768]{1,0:T(8,128)(2,1)S(1)}, u32[]{:S(2)}, u32[]{:S(2)}) collective-permute-start(bf16[16,768]{1,0:T(8,128)(2,1)S(1)} %copy.44), channel_id=1, source_target_pairs={{480,0},{0,32},{32,64},{64,96},{96,128},{128,160},{160,192},{192,2... | collective-permute-start | bytes 73736 | tf_op jit(solution)/shard_map/while/body/eval_jaxpr/ppermute | solution.py:11
  312.1 16.2 %collective-permute-start.4 = (f32[16]{0:T(128)S(1)}, f32[16]{0:T(128)S(1)}, u32[]{:S(2)}, u32[]{:S(2)}) collective-permute-start(f32[16]{0:T(128)S(1)} %copy.45), channel_id=1, source_target_pairs={{480,0},{0,32},{32,64},{64,96},{96,128},{128,160},{160,192},{192,2... | collective-permute-start | bytes 200 | tf_op jit(solution)/shard_map/while/body/eval_jaxpr/ppermute | solution.py:11
  314.5 14.5 %collective-permute-start.8 = (f32[16,768]{1,0:T(8,128)S(1)}, f32[16,768]{1,0:T(8,128)S(1)}, u32[]{:S(2)}, u32[]{:S(2)}) collective-permute-start(f32[16,768]{1,0:T(8,128)S(1)} %convolution_add_fusion.3), channel_id=1, source_target_pairs={{480,0},{0,32},{32,64},{64,96},{96,128},{128,160},{160,192},{192,2... | collective-permute-start | bytes 147464 | tf_op jit(solution)/shard_map/while/body/eval_jaxpr/ppermute | solution.py:11
  329.0 24.5 %collective-permute-start.6 = (f32[16]{0:T(128)S(1)}, f32[16]{0:T(128)S(1)}, u32[]{:S(2)}, u32[]{:S(2)}) collective-permute-start(f32[16]{0:T(128)S(1)} %copy.47), channel_id=1, source_target_pairs={{480,0},{0,32},{32,64},{64,96},{96,128},{128,160},{160,192},{192,2... | collective-permute-start | bytes 200 | tf_op jit(solution)/shard_map/while/body/eval_jaxpr/ppermute | solution.py:11
  333.1 21.2 %collective-permute-start.3 = (bf16[16,768]{1,0:T(8,128)(2,1)S(1)}, bf16[16,768]{1,0:T(8,128)(2,1)S(1)}, u32[]{:S(2)}, u32[]{:S(2)}) collective-permute-start(bf16[16,768]{1,0:T(8,128)(2,1)S(1)} %copy.44), channel_id=1, source_target_pairs={{480,0},{0,32},{32,64},{64,96},{96,128},{128,160},{160,192},{192,2... | collective-permute-start | bytes 73736 | tf_op jit(solution)/shard_map/while/body/eval_jaxpr/ppermute | solution.py:11
  337.3 16.2 %collective-permute-start.4 = (f32[16]{0:T(128)S(1)}, f32[16]{0:T(128)S(1)}, u32[]{:S(2)}, u32[]{:S(2)}) collective-permute-start(f32[16]{0:T(128)S(1)} %copy.45), channel_id=1, source_target_pairs={{480,0},{0,32},{32,64},{64,96},{96,128},{128,160},{160,192},{192,2... | collective-permute-start | bytes 200 | tf_op jit(solution)/shard_map/while/body/eval_jaxpr/ppermute | solution.py:11
  339.8 14.5 %collective-permute-start.8 = (f32[16,768]{1,0:T(8,128)S(1)}, f32[16,768]{1,0:T(8,128)S(1)}, u32[]{:S(2)}, u32[]{:S(2)}) collective-permute-start(f32[16,768]{1,0:T(8,128)S(1)} %convolution_add_fusion.3), channel_id=1, source_target_pairs={{480,0},{0,32},{32,64},{64,96},{96,128},{128,160},{160,192},{192,2... | collective-permute-start | bytes 147464 | tf_op jit(solution)/shard_map/while/body/eval_jaxpr/ppermute | solution.py:11
  354.3 24.5 %collective-permute-start.6 = (f32[16]{0:T(128)S(1)}, f32[16]{0:T(128)S(1)}, u32[]{:S(2)}, u32[]{:S(2)}) collective-permute-start(f32[16]{0:T(128)S(1)} %copy.47), channel_id=1, source_target_pairs={{480,0},{0,32},{32,64},{64,96},{96,128},{128,160},{160,192},{192,2... | collective-permute-start | bytes 200 | tf_op jit(solution)/shard_map/while/body/eval_jaxpr/ppermute | solution.py:11
  358.4 21.2 %collective-permute-start.3 = (bf16[16,768]{1,0:T(8,128)(2,1)S(1)}, bf16[16,768]{1,0:T(8,128)(2,1)S(1)}, u32[]{:S(2)}, u32[]{:S(2)}) collective-permute-start(bf16[16,768]{1,0:T(8,128)(2,1)S(1)} %copy.44), channel_id=1, source_target_pairs={{480,0},{0,32},{32,64},{64,96},{96,128},{128,160},{160,192},{192,2... | collective-permute-start | bytes 73736 | tf_op jit(solution)/shard_map/while/body/eval_jaxpr/ppermute | solution.py:11
  362.6 16.2 %collective-permute-start.4 = (f32[16]{0:T(128)S(1)}, f32[16]{0:T(128)S(1)}, u32[]{:S(2)}, u32[]{:S(2)}) collective-permute-start(f32[16]{0:T(128)S(1)} %copy.45), channel_id=1, source_target_pairs={{480,0},{0,32},{32,64},{64,96},{96,128},{128,160},{160,192},{192,2... | collective-permute-start | bytes 200 | tf_op jit(solution)/shard_map/while/body/eval_jaxpr/ppermute | solution.py:11
  365.0 14.5 %collective-permute-start.8 = (f32[16,768]{1,0:T(8,128)S(1)}, f32[16,768]{1,0:T(8,128)S(1)}, u32[]{:S(2)}, u32[]{:S(2)}) collective-permute-start(f32[16,768]{1,0:T(8,128)S(1)} %convolution_add_fusion.3), channel_id=1, source_target_pairs={{480,0},{0,32},{32,64},{64,96},{96,128},{128,160},{160,192},{192,2... | collective-permute-start | bytes 147464 | tf_op jit(solution)/shard_map/while/body/eval_jaxpr/ppermute | solution.py:11
  379.6 24.5 %collective-permute-start.6 = (f32[16]{0:T(128)S(1)}, f32[16]{0:T(128)S(1)}, u32[]{:S(2)}, u32[]{:S(2)}) collective-permute-start(f32[16]{0:T(128)S(1)} %copy.47), channel_id=1, source_target_pairs={{480,0},{0,32},{32,64},{64,96},{96,128},{128,160},{160,192},{192,2... | collective-permute-start | bytes 200 | tf_op jit(solution)/shard_map/while/body/eval_jaxpr/ppermute | solution.py:11
  383.7 21.2 %collective-permute-start.3 = (bf16[16,768]{1,0:T(8,128)(2,1)S(1)}, bf16[16,768]{1,0:T(8,128)(2,1)S(1)}, u32[]{:S(2)}, u32[]{:S(2)}) collective-permute-start(bf16[16,768]{1,0:T(8,128)(2,1)S(1)} %copy.44), channel_id=1, source_target_pairs={{480,0},{0,32},{32,64},{64,96},{96,128},{128,160},{160,192},{192,2... | collective-permute-start | bytes 73736 | tf_op jit(solution)/shard_map/while/body/eval_jaxpr/ppermute | solution.py:11
  387.9 16.2 %collective-permute-start.4 = (f32[16]{0:T(128)S(1)}, f32[16]{0:T(128)S(1)}, u32[]{:S(2)}, u32[]{:S(2)}) collective-permute-start(f32[16]{0:T(128)S(1)} %copy.45), channel_id=1, source_target_pairs={{480,0},{0,32},{32,64},{64,96},{96,128},{128,160},{160,192},{192,2... | collective-permute-start | bytes 200 | tf_op jit(solution)/shard_map/while/body/eval_jaxpr/ppermute | solution.py:11
  390.3 14.5 %collective-permute-start.8 = (f32[16,768]{1,0:T(8,128)S(1)}, f32[16,768]{1,0:T(8,128)S(1)}, u32[]{:S(2)}, u32[]{:S(2)}) collective-permute-start(f32[16,768]{1,0:T(8,128)S(1)} %convolution_add_fusion.3), channel_id=1, source_target_pairs={{480,0},{0,32},{32,64},{64,96},{96,128},{128,160},{160,192},{192,2... | collective-permute-start | bytes 147464 | tf_op jit(solution)/shard_map/while/body/eval_jaxpr/ppermute | solution.py:11
  404.8 24.5 %collective-permute-start.6 = (f32[16]{0:T(128)S(1)}, f32[16]{0:T(128)S(1)}, u32[]{:S(2)}, u32[]{:S(2)}) collective-permute-start(f32[16]{0:T(128)S(1)} %copy.47), channel_id=1, source_target_pairs={{480,0},{0,32},{32,64},{64,96},{96,128},{128,160},{160,192},{192,2... | collective-permute-start | bytes 200 | tf_op jit(solution)/shard_map/while/body/eval_jaxpr/ppermute | solution.py:11
  408.9 21.2 %collective-permute-start.3 = (bf16[16,768]{1,0:T(8,128)(2,1)S(1)}, bf16[16,768]{1,0:T(8,128)(2,1)S(1)}, u32[]{:S(2)}, u32[]{:S(2)}) collective-permute-start(bf16[16,768]{1,0:T(8,128)(2,1)S(1)} %copy.44), channel_id=1, source_target_pairs={{480,0},{0,32},{32,64},{64,96},{96,128},{128,160},{160,192},{192,2... | collective-permute-start | bytes 73736 | tf_op jit(solution)/shard_map/while/body/eval_jaxpr/ppermute | solution.py:11
  413.1 16.2 %collective-permute-start.4 = (f32[16]{0:T(128)S(1)}, f32[16]{0:T(128)S(1)}, u32[]{:S(2)}, u32[]{:S(2)}) collective-permute-start(f32[16]{0:T(128)S(1)} %copy.45), channel_id=1, source_target_pairs={{480,0},{0,32},{32,64},{64,96},{96,128},{128,160},{160,192},{192,2... | collective-permute-start | bytes 200 | tf_op jit(solution)/shard_map/while/body/eval_jaxpr/ppermute | solution.py:11
  415.6 14.5 %collective-permute-start.8 = (f32[16,768]{1,0:T(8,128)S(1)}, f32[16,768]{1,0:T(8,128)S(1)}, u32[]{:S(2)}, u32[]{:S(2)}) collective-permute-start(f32[16,768]{1,0:T(8,128)S(1)} %convolution_add_fusion.3), channel_id=1, source_target_pairs={{480,0},{0,32},{32,64},{64,96},{96,128},{128,160},{160,192},{192,2... | collective-permute-start | bytes 147464 | tf_op jit(solution)/shard_map/while/body/eval_jaxpr/ppermute | solution.py:11
  430.1 24.5 %collective-permute-start.6 = (f32[16]{0:T(128)S(1)}, f32[16]{0:T(128)S(1)}, u32[]{:S(2)}, u32[]{:S(2)}) collective-permute-start(f32[16]{0:T(128)S(1)} %copy.47), channel_id=1, source_target_pairs={{480,0},{0,32},{32,64},{64,96},{96,128},{128,160},{160,192},{192,2... | collective-permute-start | bytes 200 | tf_op jit(solution)/shard_map/while/body/eval_jaxpr/ppermute | solution.py:11
  434.2 21.2 %collective-permute-start.3 = (bf16[16,768]{1,0:T(8,128)(2,1)S(1)}, bf16[16,768]{1,0:T(8,128)(2,1)S(1)}, u32[]{:S(2)}, u32[]{:S(2)}) collective-permute-start(bf16[16,768]{1,0:T(8,128)(2,1)S(1)} %copy.44), channel_id=1, source_target_pairs={{480,0},{0,32},{32,64},{64,96},{96,128},{128,160},{160,192},{192,2... | collective-permute-start | bytes 73736 | tf_op jit(solution)/shard_map/while/body/eval_jaxpr/ppermute | solution.py:11
  438.4 16.2 %collective-permute-start.4 = (f32[16]{0:T(128)S(1)}, f32[16]{0:T(128)S(1)}, u32[]{:S(2)}, u32[]{:S(2)}) collective-permute-start(f32[16]{0:T(128)S(1)} %copy.45), channel_id=1, source_target_pairs={{480,0},{0,32},{32,64},{64,96},{96,128},{128,160},{160,192},{192,2... | collective-permute-start | bytes 200 | tf_op jit(solution)/shard_map/while/body/eval_jaxpr/ppermute | solution.py:11
  440.8 14.5 %collective-permute-start.8 = (f32[16,768]{1,0:T(8,128)S(1)}, f32[16,768]{1,0:T(8,128)S(1)}, u32[]{:S(2)}, u32[]{:S(2)}) collective-permute-start(f32[16,768]{1,0:T(8,128)S(1)} %convolution_add_fusion.3), channel_id=1, source_target_pairs={{480,0},{0,32},{32,64},{64,96},{96,128},{128,160},{160,192},{192,2... | collective-permute-start | bytes 147464 | tf_op jit(solution)/shard_map/while/body/eval_jaxpr/ppermute | solution.py:11
  455.4 24.5 %collective-permute-start.6 = (f32[16]{0:T(128)S(1)}, f32[16]{0:T(128)S(1)}, u32[]{:S(2)}, u32[]{:S(2)}) collective-permute-start(f32[16]{0:T(128)S(1)} %copy.47), channel_id=1, source_target_pairs={{480,0},{0,32},{32,64},{64,96},{96,128},{128,160},{160,192},{192,2... | collective-permute-start | bytes 200 | tf_op jit(solution)/shard_map/while/body/eval_jaxpr/ppermute | solution.py:11
  459.5 21.2 %collective-permute-start.3 = (bf16[16,768]{1,0:T(8,128)(2,1)S(1)}, bf16[16,768]{1,0:T(8,128)(2,1)S(1)}, u32[]{:S(2)}, u32[]{:S(2)}) collective-permute-start(bf16[16,768]{1,0:T(8,128)(2,1)S(1)} %copy.44), channel_id=1, source_target_pairs={{480,0},{0,32},{32,64},{64,96},{96,128},{128,160},{160,192},{192,2... | collective-permute-start | bytes 73736 | tf_op jit(solution)/shard_map/while/body/eval_jaxpr/ppermute | solution.py:11
  463.7 16.2 %collective-permute-start.4 = (f32[16]{0:T(128)S(1)}, f32[16]{0:T(128)S(1)}, u32[]{:S(2)}, u32[]{:S(2)}) collective-permute-start(f32[16]{0:T(128)S(1)} %copy.45), channel_id=1, source_target_pairs={{480,0},{0,32},{32,64},{64,96},{96,128},{128,160},{160,192},{192,2... | collective-permute-start | bytes 200 | tf_op jit(solution)/shard_map/while/body/eval_jaxpr/ppermute | solution.py:11
  466.1 14.5 %collective-permute-start.8 = (f32[16,768]{1,0:T(8,128)S(1)}, f32[16,768]{1,0:T(8,128)S(1)}, u32[]{:S(2)}, u32[]{:S(2)}) collective-permute-start(f32[16,768]{1,0:T(8,128)S(1)} %convolution_add_fusion.3), channel_id=1, source_target_pairs={{480,0},{0,32},{32,64},{64,96},{96,128},{128,160},{160,192},{192,2... | collective-permute-start | bytes 147464 | tf_op jit(solution)/shard_map/while/body/eval_jaxpr/ppermute | solution.py:11
  480.6 24.5 %collective-permute-start.6 = (f32[16]{0:T(128)S(1)}, f32[16]{0:T(128)S(1)}, u32[]{:S(2)}, u32[]{:S(2)}) collective-permute-start(f32[16]{0:T(128)S(1)} %copy.47), channel_id=1, source_target_pairs={{480,0},{0,32},{32,64},{64,96},{96,128},{128,160},{160,192},{192,2... | collective-permute-start | bytes 200 | tf_op jit(solution)/shard_map/while/body/eval_jaxpr/ppermute | solution.py:11
  484.7 21.2 %collective-permute-start.3 = (bf16[16,768]{1,0:T(8,128)(2,1)S(1)}, bf16[16,768]{1,0:T(8,128)(2,1)S(1)}, u32[]{:S(2)}, u32[]{:S(2)}) collective-permute-start(bf16[16,768]{1,0:T(8,128)(2,1)S(1)} %copy.44), channel_id=1, source_target_pairs={{480,0},{0,32},{32,64},{64,96},{96,128},{128,160},{160,192},{192,2... | collective-permute-start | bytes 73736 | tf_op jit(solution)/shard_map/while/body/eval_jaxpr/ppermute | solution.py:11
  488.9 16.2 %collective-permute-start.4 = (f32[16]{0:T(128)S(1)}, f32[16]{0:T(128)S(1)}, u32[]{:S(2)}, u32[]{:S(2)}) collective-permute-start(f32[16]{0:T(128)S(1)} %copy.45), channel_id=1, source_target_pairs={{480,0},{0,32},{32,64},{64,96},{96,128},{128,160},{160,192},{192,2... | collective-permute-start | bytes 200 | tf_op jit(solution)/shard_map/while/body/eval_jaxpr/ppermute | solution.py:11
  491.4 14.5 %collective-permute-start.8 = (f32[16,768]{1,0:T(8,128)S(1)}, f32[16,768]{1,0:T(8,128)S(1)}, u32[]{:S(2)}, u32[]{:S(2)}) collective-permute-start(f32[16,768]{1,0:T(8,128)S(1)} %convolution_add_fusion.3), channel_id=1, source_target_pairs={{480,0},{0,32},{32,64},{64,96},{96,128},{128,160},{160,192},{192,2... | collective-permute-start | bytes 147464 | tf_op jit(solution)/shard_map/while/body/eval_jaxpr/ppermute | solution.py:11
  505.9 24.5 %collective-permute-start.6 = (f32[16]{0:T(128)S(1)}, f32[16]{0:T(128)S(1)}, u32[]{:S(2)}, u32[]{:S(2)}) collective-permute-start(f32[16]{0:T(128)S(1)} %copy.47), channel_id=1, source_target_pairs={{480,0},{0,32},{32,64},{64,96},{96,128},{128,160},{160,192},{192,2... | collective-permute-start | bytes 200 | tf_op jit(solution)/shard_map/while/body/eval_jaxpr/ppermute | solution.py:11
  510.0 21.2 %collective-permute-start.3 = (bf16[16,768]{1,0:T(8,128)(2,1)S(1)}, bf16[16,768]{1,0:T(8,128)(2,1)S(1)}, u32[]{:S(2)}, u32[]{:S(2)}) collective-permute-start(bf16[16,768]{1,0:T(8,128)(2,1)S(1)} %copy.44), channel_id=1, source_target_pairs={{480,0},{0,32},{32,64},{64,96},{96,128},{128,160},{160,192},{192,2... | collective-permute-start | bytes 73736 | tf_op jit(solution)/shard_map/while/body/eval_jaxpr/ppermute | solution.py:11
  514.2 16.2 %collective-permute-start.4 = (f32[16]{0:T(128)S(1)}, f32[16]{0:T(128)S(1)}, u32[]{:S(2)}, u32[]{:S(2)}) collective-permute-start(f32[16]{0:T(128)S(1)} %copy.45), channel_id=1, source_target_pairs={{480,0},{0,32},{32,64},{64,96},{96,128},{128,160},{160,192},{192,2... | collective-permute-start | bytes 200 | tf_op jit(solution)/shard_map/while/body/eval_jaxpr/ppermute | solution.py:11
  516.6 14.5 %collective-permute-start.8 = (f32[16,768]{1,0:T(8,128)S(1)}, f32[16,768]{1,0:T(8,128)S(1)}, u32[]{:S(2)}, u32[]{:S(2)}) collective-permute-start(f32[16,768]{1,0:T(8,128)S(1)} %convolution_add_fusion.3), channel_id=1, source_target_pairs={{480,0},{0,32},{32,64},{64,96},{96,128},{128,160},{160,192},{192,2... | collective-permute-start | bytes 147464 | tf_op jit(solution)/shard_map/while/body/eval_jaxpr/ppermute | solution.py:11
  531.2 24.5 %collective-permute-start.6 = (f32[16]{0:T(128)S(1)}, f32[16]{0:T(128)S(1)}, u32[]{:S(2)}, u32[]{:S(2)}) collective-permute-start(f32[16]{0:T(128)S(1)} %copy.47), channel_id=1, source_target_pairs={{480,0},{0,32},{32,64},{64,96},{96,128},{128,160},{160,192},{192,2... | collective-permute-start | bytes 200 | tf_op jit(solution)/shard_map/while/body/eval_jaxpr/ppermute | solution.py:11
  535.3 21.2 %collective-permute-start.3 = (bf16[16,768]{1,0:T(8,128)(2,1)S(1)}, bf16[16,768]{1,0:T(8,128)(2,1)S(1)}, u32[]{:S(2)}, u32[]{:S(2)}) collective-permute-start(bf16[16,768]{1,0:T(8,128)(2,1)S(1)} %copy.44), channel_id=1, source_target_pairs={{480,0},{0,32},{32,64},{64,96},{96,128},{128,160},{160,192},{192,2... | collective-permute-start | bytes 73736 | tf_op jit(solution)/shard_map/while/body/eval_jaxpr/ppermute | solution.py:11
  539.5 16.2 %collective-permute-start.4 = (f32[16]{0:T(128)S(1)}, f32[16]{0:T(128)S(1)}, u32[]{:S(2)}, u32[]{:S(2)}) collective-permute-start(f32[16]{0:T(128)S(1)} %copy.45), channel_id=1, source_target_pairs={{480,0},{0,32},{32,64},{64,96},{96,128},{128,160},{160,192},{192,2... | collective-permute-start | bytes 200 | tf_op jit(solution)/shard_map/while/body/eval_jaxpr/ppermute | solution.py:11
  541.9 14.5 %collective-permute-start.8 = (f32[16,768]{1,0:T(8,128)S(1)}, f32[16,768]{1,0:T(8,128)S(1)}, u32[]{:S(2)}, u32[]{:S(2)}) collective-permute-start(f32[16,768]{1,0:T(8,128)S(1)} %convolution_add_fusion.3), channel_id=1, source_target_pairs={{480,0},{0,32},{32,64},{64,96},{96,128},{128,160},{160,192},{192,2... | collective-permute-start | bytes 147464 | tf_op jit(solution)/shard_map/while/body/eval_jaxpr/ppermute | solution.py:11
  556.4 24.5 %collective-permute-start.6 = (f32[16]{0:T(128)S(1)}, f32[16]{0:T(128)S(1)}, u32[]{:S(2)}, u32[]{:S(2)}) collective-permute-start(f32[16]{0:T(128)S(1)} %copy.47), channel_id=1, source_target_pairs={{480,0},{0,32},{32,64},{64,96},{96,128},{128,160},{160,192},{192,2... | collective-permute-start | bytes 200 | tf_op jit(solution)/shard_map/while/body/eval_jaxpr/ppermute | solution.py:11
  560.5 21.2 %collective-permute-start.3 = (bf16[16,768]{1,0:T(8,128)(2,1)S(1)}, bf16[16,768]{1,0:T(8,128)(2,1)S(1)}, u32[]{:S(2)}, u32[]{:S(2)}) collective-permute-start(bf16[16,768]{1,0:T(8,128)(2,1)S(1)} %copy.44), channel_id=1, source_target_pairs={{480,0},{0,32},{32,64},{64,96},{96,128},{128,160},{160,192},{192,2... | collective-permute-start | bytes 73736 | tf_op jit(solution)/shard_map/while/body/eval_jaxpr/ppermute | solution.py:11
  564.7 16.2 %collective-permute-start.4 = (f32[16]{0:T(128)S(1)}, f32[16]{0:T(128)S(1)}, u32[]{:S(2)}, u32[]{:S(2)}) collective-permute-start(f32[16]{0:T(128)S(1)} %copy.45), channel_id=1, source_target_pairs={{480,0},{0,32},{32,64},{64,96},{96,128},{128,160},{160,192},{192,2... | collective-permute-start | bytes 200 | tf_op jit(solution)/shard_map/while/body/eval_jaxpr/ppermute | solution.py:11
  567.2 14.5 %collective-permute-start.8 = (f32[16,768]{1,0:T(8,128)S(1)}, f32[16,768]{1,0:T(8,128)S(1)}, u32[]{:S(2)}, u32[]{:S(2)}) collective-permute-start(f32[16,768]{1,0:T(8,128)S(1)} %convolution_add_fusion.3), channel_id=1, source_target_pairs={{480,0},{0,32},{32,64},{64,96},{96,128},{128,160},{160,192},{192,2... | collective-permute-start | bytes 147464 | tf_op jit(solution)/shard_map/while/body/eval_jaxpr/ppermute | solution.py:11
  581.7 24.5 %collective-permute-start.6 = (f32[16]{0:T(128)S(1)}, f32[16]{0:T(128)S(1)}, u32[]{:S(2)}, u32[]{:S(2)}) collective-permute-start(f32[16]{0:T(128)S(1)} %copy.47), channel_id=1, source_target_pairs={{480,0},{0,32},{32,64},{64,96},{96,128},{128,160},{160,192},{192,2... | collective-permute-start | bytes 200 | tf_op jit(solution)/shard_map/while/body/eval_jaxpr/ppermute | solution.py:11
  585.8 21.2 %collective-permute-start.3 = (bf16[16,768]{1,0:T(8,128)(2,1)S(1)}, bf16[16,768]{1,0:T(8,128)(2,1)S(1)}, u32[]{:S(2)}, u32[]{:S(2)}) collective-permute-start(bf16[16,768]{1,0:T(8,128)(2,1)S(1)} %copy.44), channel_id=1, source_target_pairs={{480,0},{0,32},{32,64},{64,96},{96,128},{128,160},{160,192},{192,2... | collective-permute-start | bytes 73736 | tf_op jit(solution)/shard_map/while/body/eval_jaxpr/ppermute | solution.py:11
  590.0 16.2 %collective-permute-start.4 = (f32[16]{0:T(128)S(1)}, f32[16]{0:T(128)S(1)}, u32[]{:S(2)}, u32[]{:S(2)}) collective-permute-start(f32[16]{0:T(128)S(1)} %copy.45), channel_id=1, source_target_pairs={{480,0},{0,32},{32,64},{64,96},{96,128},{128,160},{160,192},{192,2... | collective-permute-start | bytes 200 | tf_op jit(solution)/shard_map/while/body/eval_jaxpr/ppermute | solution.py:11
  592.4 14.5 %collective-permute-start.8 = (f32[16,768]{1,0:T(8,128)S(1)}, f32[16,768]{1,0:T(8,128)S(1)}, u32[]{:S(2)}, u32[]{:S(2)}) collective-permute-start(f32[16,768]{1,0:T(8,128)S(1)} %convolution_add_fusion.3), channel_id=1, source_target_pairs={{480,0},{0,32},{32,64},{64,96},{96,128},{128,160},{160,192},{192,2... | collective-permute-start | bytes 147464 | tf_op jit(solution)/shard_map/while/body/eval_jaxpr/ppermute | solution.py:11
  607.0 24.5 %collective-permute-start.6 = (f32[16]{0:T(128)S(1)}, f32[16]{0:T(128)S(1)}, u32[]{:S(2)}, u32[]{:S(2)}) collective-permute-start(f32[16]{0:T(128)S(1)} %copy.47), channel_id=1, source_target_pairs={{480,0},{0,32},{32,64},{64,96},{96,128},{128,160},{160,192},{192,2... | collective-permute-start | bytes 200 | tf_op jit(solution)/shard_map/while/body/eval_jaxpr/ppermute | solution.py:11
  611.1 21.2 %collective-permute-start.3 = (bf16[16,768]{1,0:T(8,128)(2,1)S(1)}, bf16[16,768]{1,0:T(8,128)(2,1)S(1)}, u32[]{:S(2)}, u32[]{:S(2)}) collective-permute-start(bf16[16,768]{1,0:T(8,128)(2,1)S(1)} %copy.44), channel_id=1, source_target_pairs={{480,0},{0,32},{32,64},{64,96},{96,128},{128,160},{160,192},{192,2... | collective-permute-start | bytes 73736 | tf_op jit(solution)/shard_map/while/body/eval_jaxpr/ppermute | solution.py:11
  615.3 16.2 %collective-permute-start.4 = (f32[16]{0:T(128)S(1)}, f32[16]{0:T(128)S(1)}, u32[]{:S(2)}, u32[]{:S(2)}) collective-permute-start(f32[16]{0:T(128)S(1)} %copy.45), channel_id=1, source_target_pairs={{480,0},{0,32},{32,64},{64,96},{96,128},{128,160},{160,192},{192,2... | collective-permute-start | bytes 200 | tf_op jit(solution)/shard_map/while/body/eval_jaxpr/ppermute | solution.py:11
  617.7 14.5 %collective-permute-start.8 = (f32[16,768]{1,0:T(8,128)S(1)}, f32[16,768]{1,0:T(8,128)S(1)}, u32[]{:S(2)}, u32[]{:S(2)}) collective-permute-start(f32[16,768]{1,0:T(8,128)S(1)} %convolution_add_fusion.3), channel_id=1, source_target_pairs={{480,0},{0,32},{32,64},{64,96},{96,128},{128,160},{160,192},{192,2... | collective-permute-start | bytes 147464 | tf_op jit(solution)/shard_map/while/body/eval_jaxpr/ppermute | solution.py:11
  (87 other events, 619.2 us)
Sparse Core Ops, SparseCore 0:
  651.5 482.4 all-reduce.1
where the time goes:
time: 1150 us; the launch traced here: 1140 us
  waiting for transfers between devices  542 us (47%)
  starting transfers between devices  523 us (45%)
  local copies, waits for them, and re-layouts  30.9 us (3%)
  matrix products  27 us (2%)
  between operations  14.1 us (1%)
    ppermute x144, starting transfers between devices, shifted(): return lax.ppermute(block, axis, route)  523 us
    psum x1, waiting for transfers between devices, per_device(): book_total = lax.psum(book_grad, ('db', 'pb'))  481 us
    ppermute x144, waiting for transfers between devices, shifted(): return lax.ppermute(block, axis, route)  60.2 us
  transfers between devices with their start and end apart: 145, of which 49 were waited for; matrix products, arithmetic and copies ran while one was open for 2% of the time, Pallas kernels for 0%

commit v1 on v0

--- a/solution.py
+++ b/solution.py
@@ -158,7 +158,7 @@
     grad_queries = final_state[5]
     book_grad = book_part(passage_codes, final_state[6], codebooks)
     query_loss = loss_weight * (log_total - chosen)
-    book_total = lax.psum(book_grad, ("db", "pb"))
+    book_total = lax.psum(lax.psum(book_grad, "pb"), "db")
     return (query_loss, grad_queries, book_total)
 
 

time: 1150 us -> 1080 us (0.939)
  the two profiles are of different devices: /device:TPU:2 before, /device:TPU:1 now
where the time goes in v1:
time: 1080 us
  waiting for transfers between devices  633 us (59%)
  starting transfers between devices  368 us (34%)
  local copies, waits for them, and re-layouts  30.9 us (3%)
  matrix products  27 us (2%)
  between operations  14.1 us (1%)
    psum x2, waiting for transfers between devices, per_device(): book_total = lax.psum(lax.psum(book_grad, 'pb'), 'db')  414 us
    ppermute x144, starting transfers between devices, shifted(): return lax.ppermute(block, axis, route)  368 us
    ppermute x144, waiting for transfers between devices, shifted(): return lax.ppermute(block, axis, route)  219 us
    eq x32, local copies, waits for them, and re-layouts, code_table(): return (levels[None, :, None] == code_rows[:, None, :]).astype(jnp.bfloat16)  22 us
  transfers between devices with their start and end apart: 146, of which 66 were waited for; matrix products, arithmetic and copies ran while one was open for 2% of the time, Pallas kernels for 0%

profile of v1, /device:TPU:1, one launch (start us, length us, event | category | flops | bytes accessed | tf_op | source)
XLA Modules:
  0.0 1079.4 jit_solution(7554915710560477680)
XLA Ops:
  9.2 14.4 %while.57 = (s32[]{:T(128)}, bf16[16,4,12,128]{3,2,1,0:T(8,128)(2,1)S(1)}, bf16[16,4,12,256]{3,2,1,0:T(8,128)(2,1)S(1)}, s32[16,4,128]{2,1,0:T(4,128)}, s32[]{:T(128)}) while((s32[]{:T(128)}, bf16[16,4,12,128]{3,2,1,0:T(8,128)(2,1)S(1)}, bf16[16,4,12,256]{3,2,1,0:T(8,128)(2,1)S(1)}, s32[16,4,128]{2,1,0:T(4,128)}, s32[]{:T(128)}) %tuple.92), condition=%wide.region_1.2_spmd, body=%wide.region_0.1_spmd.sunk | while | flops 3276802 | bytes 72769 | solution.py:30
  23.6 206.1 %while.58 = (s32[]{:T(128)}, bf16[16,768]{1,0:T(8,128)(2,1)S(1)}, f32[16]{0:T(128)S(1)}, f32[16]{0:T(128)S(1)}, bf16[768,128]{1,0:T(8,128)(2,1)S(1)}, /*index=5*/s32[]{:T(128)}) while((s32[]{:T(128)}, bf16[16,768]{1,0:T(8,128)(2,1)S(1)}, f32[16]{0:T(128)S(1)}, f32[16]{0:T(128)S(1)}, bf16[768,128]{1,0:T(8,128)(2,1)S(1)}, ...), condition=%wide.region_5.6_spmd, body=%wide.region_2.5_spmd.sunk | while | flops 3153954 | bytes 386557 | solution.py:102
  23.6 4.5 collective-permute-start
  30.5 3.5 collective-permute-start.2
  44.5 3.5 collective-permute-done.1
  57.0 3.9 collective-permute-done.1
  67.3 4.0 collective-permute-start.2
  80.1 4.0 collective-permute-start.2
  93.0 4.0 collective-permute-start.2
  105.8 4.0 collective-permute-start.2
  118.6 4.0 collective-permute-start.2
  131.4 4.0 collective-permute-start.2
  144.2 4.0 collective-permute-start.2
  157.1 4.0 collective-permute-start.2
  169.9 4.0 collective-permute-start.2
  182.7 4.0 collective-permute-start.2
  195.5 4.0 collective-permute-start.2
  208.4 4.0 collective-permute-start.2
  221.2 4.0 collective-permute-start.2
  231.5 404.3 %while.60 = (s32[]{:T(128)}, bf16[16,768]{1,0:T(8,128)(2,1)S(1)}, f32[16]{0:T(128)S(1)}, f32[16]{0:T(128)S(1)}, f32[16]{0:T(128)S(1)}, /*index=5*/f32[16]{0:T(12...) while((s32[]{:T(128)}, bf16[16,768]{1,0:T(8,128)(2,1)S(1)}, ...), condition=%wide.region_8.9_spmd.clone, body=%wide.region_6.8_spmd.clone.sunk | while | flops 9683203 | bytes 1700275 | solution.py:156
  235.4 4.0 collective-permute-start.4
  239.9 3.3 collective-permute-start.8
  243.3 4.2 collective-permute-start.7
  248.3 4.0 collective-permute-start.5
  252.3 4.4 collective-permute-done.5
  260.7 4.0 collective-permute-start.4
  269.5 4.1 collective-permute-done.7
  275.5 6.6 collective-permute-done.5
  284.0 3.1 collective-permute-start.3
  287.1 4.2 collective-permute-start.4
  300.8 6.6 collective-permute-done.5
  309.3 3.1 collective-permute-start.3
  312.4 4.2 collective-permute-start.4
  326.0 6.6 collective-permute-done.5
  334.5 3.1 collective-permute-start.3
  337.6 4.2 collective-permute-start.4
  351.3 6.6 collective-permute-done.5
  359.8 3.1 collective-permute-start.3
  362.9 4.2 collective-permute-start.4
  376.6 6.6 collective-permute-done.5
  385.1 3.1 collective-permute-start.3
  388.2 4.2 collective-permute-start.4
  401.8 6.6 collective-permute-done.5
  413.5 4.2 collective-permute-start.4
  427.1 6.6 collective-permute-done.5
  438.7 4.2 collective-permute-start.4
  452.4 6.6 collective-permute-done.5
  464.0 4.2 collective-permute-start.4
  477.6 6.6 collective-permute-done.5
  489.3 4.2 collective-permute-start.4
  502.9 6.6 collective-permute-done.5
  514.5 4.2 collective-permute-start.4
  528.2 6.6 collective-permute-done.5
  539.8 4.2 collective-permute-start.4
  553.4 6.6 collective-permute-done.5
  565.1 4.2 collective-permute-start.4
  578.7 6.6 collective-permute-done.5
  590.3 4.2 collective-permute-start.4
  604.0 6.6 collective-permute-done.5
  615.6 4.2 collective-permute-start.4
  629.2 6.6 collective-permute-done.5
  636.0 17.6 %while.59 = (s32[]{:T(128)}, f32[16,4,12,256]{3,2,1,0:T(8,128)S(1)}, f32[16,4,12,128]{3,2,1,0:T(8,128)S(1)}, s32[16,4,128]{2,1,0:T(4,128)}, s32[]{:T(128)}) while((s32[]{:T(128)}, f32[16,4,12,256]{3,2,1,0:T(8,128)S(1)}, f32[16,4,12,128]{3,2,1,0:T(8,128)S(1)}, s32[16,4,128]{2,1,0:T(4,128)}, s32[]{:T(128)}) %tuple.93), condition=%wide.region_10.11_spmd, body=%wide.region_9.10_spmd.sunk | while | flops 6590466 | bytes 238661 | solution.py:49
  655.0 241.5 %all-reduce.3.cloned.1.call-done = f32[64,12,256]{2,0,1:T(8,128)} async-done(((f32[64,12,256]{2,0,1:T(8,128)}), f32[64,12,256]{2,0,1:T(8,128)}) %all-reduce.3.cloned.1.call-update) | async-done | bytes 786448 | tf_op jit(solution)/shard_map/psum | solution.py:161
  897.7 172.2 %all-reduce.5.cloned.1.call-done = f32[64,12,256]{2,0,1:T(8,128)} async-done(((f32[64,12,256]{2,0,1:T(8,128)}), f32[64,12,256]{2,0,1:T(8,128)}) %all-reduce.5.cloned.1.call-update) | async-done | bytes 786448 | tf_op jit(solution)/shard_map/psum | solution.py:161
  (585 shorter events, 380.5 us)
Async XLA Ops:
  7.2 889.4 %all-reduce.3.cloned.1.call-start = ((), (), s32[]{:S(2)}) async-start(), calls=%async_computation | async-start | bytes 1572864 | tf_op jit(solution)/shard_map/psum | solution.py:161
  23.6 13.7 %collective-permute-start = (bf16[16,768]{1,0:T(8,128)(2,1)S(1)}, bf16[16,768]{1,0:T(8,128)(2,1)S(1)}, u32[]{:S(2)}, u32[]{:S(2)}) collective-permute-start(bf16[16,768]{1,0:T(8,128)(2,1)S(1)} %copy.28), channel_id=1, source_target_pairs={{480,0},{0,32},{32,64},{64,96},{96,128},{128,160},{160,192},{192,2... | collective-permute-start | bytes 73736 | tf_op jit(solution)/shard_map/while/body/eval_jaxpr/ppermute | solution.py:11
  231.5 20.8 %collective-permute-start.6 = (f32[16]{0:T(128)S(1)}, f32[16]{0:T(128)S(1)}, u32[]{:S(2)}, u32[]{:S(2)}) collective-permute-start(f32[16]{0:T(128)S(1)} %copy.47), channel_id=1, source_target_pairs={{480,0},{0,32},{32,64},{64,96},{96,128},{128,160},{160,192},{192,2... | collective-permute-start | bytes 200 | tf_op jit(solution)/shard_map/while/body/eval_jaxpr/ppermute | solution.py:11
  233.5 23.3 %collective-permute-start.3 = (bf16[16,768]{1,0:T(8,128)(2,1)S(1)}, bf16[16,768]{1,0:T(8,128)(2,1)S(1)}, u32[]{:S(2)}, u32[]{:S(2)}) collective-permute-start(bf16[16,768]{1,0:T(8,128)(2,1)S(1)} %copy.44), channel_id=1, source_target_pairs={{480,0},{0,32},{32,64},{64,96},{96,128},{128,160},{160,192},{192,2... | collective-permute-start | bytes 73736 | tf_op jit(solution)/shard_map/while/body/eval_jaxpr/ppermute | solution.py:11
  235.4 16.9 %collective-permute-start.4 = (f32[16]{0:T(128)S(1)}, f32[16]{0:T(128)S(1)}, u32[]{:S(2)}, u32[]{:S(2)}) collective-permute-start(f32[16]{0:T(128)S(1)} %copy.45), channel_id=1, source_target_pairs={{480,0},{0,32},{32,64},{64,96},{96,128},{128,160},{160,192},{192,2... | collective-permute-start | bytes 200 | tf_op jit(solution)/shard_map/while/body/eval_jaxpr/ppermute | solution.py:11
  239.9 16.8 %collective-permute-start.8 = (f32[16,768]{1,0:T(8,128)S(1)}, f32[16,768]{1,0:T(8,128)S(1)}, u32[]{:S(2)}, u32[]{:S(2)}) collective-permute-start(f32[16,768]{1,0:T(8,128)S(1)} %convolution_add_fusion.3), channel_id=1, source_target_pairs={{480,0},{0,32},{32,64},{64,96},{96,128},{128,160},{160,192},{192,2... | collective-permute-start | bytes 147464 | tf_op jit(solution)/shard_map/while/body/eval_jaxpr/ppermute | solution.py:11
  256.8 18.7 %collective-permute-start.6 = (f32[16]{0:T(128)S(1)}, f32[16]{0:T(128)S(1)}, u32[]{:S(2)}, u32[]{:S(2)}) collective-permute-start(f32[16]{0:T(128)S(1)} %copy.47), channel_id=1, source_target_pairs={{480,0},{0,32},{32,64},{64,96},{96,128},{128,160},{160,192},{192,2... | collective-permute-start | bytes 200 | tf_op jit(solution)/shard_map/while/body/eval_jaxpr/ppermute | solution.py:11
  258.7 23.3 %collective-permute-start.3 = (bf16[16,768]{1,0:T(8,128)(2,1)S(1)}, bf16[16,768]{1,0:T(8,128)(2,1)S(1)}, u32[]{:S(2)}, u32[]{:S(2)}) collective-permute-start(bf16[16,768]{1,0:T(8,128)(2,1)S(1)} %copy.44), channel_id=1, source_target_pairs={{480,0},{0,32},{32,64},{64,96},{96,128},{128,160},{160,192},{192,2... | collective-permute-start | bytes 73736 | tf_op jit(solution)/shard_map/while/body/eval_jaxpr/ppermute | solution.py:11
  260.7 14.8 %collective-permute-start.4 = (f32[16]{0:T(128)S(1)}, f32[16]{0:T(128)S(1)}, u32[]{:S(2)}, u32[]{:S(2)}) collective-permute-start(f32[16]{0:T(128)S(1)} %copy.45), channel_id=1, source_target_pairs={{480,0},{0,32},{32,64},{64,96},{96,128},{128,160},{160,192},{192,2... | collective-permute-start | bytes 200 | tf_op jit(solution)/shard_map/while/body/eval_jaxpr/ppermute | solution.py:11
  265.2 16.8 %collective-permute-start.8 = (f32[16,768]{1,0:T(8,128)S(1)}, f32[16,768]{1,0:T(8,128)S(1)}, u32[]{:S(2)}, u32[]{:S(2)}) collective-permute-start(f32[16,768]{1,0:T(8,128)S(1)} %convolution_add_fusion.3), channel_id=1, source_target_pairs={{480,0},{0,32},{32,64},{64,96},{96,128},{128,160},{160,192},{192,2... | collective-permute-start | bytes 147464 | tf_op jit(solution)/shard_map/while/body/eval_jaxpr/ppermute | solution.py:11
  282.1 18.7 %collective-permute-start.6 = (f32[16]{0:T(128)S(1)}, f32[16]{0:T(128)S(1)}, u32[]{:S(2)}, u32[]{:S(2)}) collective-permute-start(f32[16]{0:T(128)S(1)} %copy.47), channel_id=1, source_target_pairs={{480,0},{0,32},{32,64},{64,96},{96,128},{128,160},{160,192},{192,2... | collective-permute-start | bytes 200 | tf_op jit(solution)/shard_map/while/body/eval_jaxpr/ppermute | solution.py:11
  284.0 23.3 %collective-permute-start.3 = (bf16[16,768]{1,0:T(8,128)(2,1)S(1)}, bf16[16,768]{1,0:T(8,128)(2,1)S(1)}, u32[]{:S(2)}, u32[]{:S(2)}) collective-permute-start(bf16[16,768]{1,0:T(8,128)(2,1)S(1)} %copy.44), channel_id=1, source_target_pairs={{480,0},{0,32},{32,64},{64,96},{96,128},{128,160},{160,192},{192,2... | collective-permute-start | bytes 73736 | tf_op jit(solution)/shard_map/while/body/eval_jaxpr/ppermute | solution.py:11
  287.1 13.6 %collective-permute-start.4 = (f32[16]{0:T(128)S(1)}, f32[16]{0:T(128)S(1)}, u32[]{:S(2)}, u32[]{:S(2)}) collective-permute-start(f32[16]{0:T(128)S(1)} %copy.45), channel_id=1, source_target_pairs={{480,0},{0,32},{32,64},{64,96},{96,128},{128,160},{160,192},{192,2... | collective-permute-start | bytes 200 | tf_op jit(solution)/shard_map/while/body/eval_jaxpr/ppermute | solution.py:11
  291.8 15.5 %collective-permute-start.8 = (f32[16,768]{1,0:T(8,128)S(1)}, f32[16,768]{1,0:T(8,128)S(1)}, u32[]{:S(2)}, u32[]{:S(2)}) collective-permute-start(f32[16,768]{1,0:T(8,128)S(1)} %convolution_add_fusion.3), channel_id=1, source_target_pairs={{480,0},{0,32},{32,64},{64,96},{96,128},{128,160},{160,192},{192,2... | collective-permute-start | bytes 147464 | tf_op jit(solution)/shard_map/while/body/eval_jaxpr/ppermute | solution.py:11
  307.3 18.7 %collective-permute-start.6 = (f32[16]{0:T(128)S(1)}, f32[16]{0:T(128)S(1)}, u32[]{:S(2)}, u32[]{:S(2)}) collective-permute-start(f32[16]{0:T(128)S(1)} %copy.47), channel_id=1, source_target_pairs={{480,0},{0,32},{32,64},{64,96},{96,128},{128,160},{160,192},{192,2... | collective-permute-start | bytes 200 | tf_op jit(solution)/shard_map/while/body/eval_jaxpr/ppermute | solution.py:11
  309.3 23.3 %collective-permute-start.3 = (bf16[16,768]{1,0:T(8,128)(2,1)S(1)}, bf16[16,768]{1,0:T(8,128)(2,1)S(1)}, u32[]{:S(2)}, u32[]{:S(2)}) collective-permute-start(bf16[16,768]{1,0:T(8,128)(2,1)S(1)} %copy.44), channel_id=1, source_target_pairs={{480,0},{0,32},{32,64},{64,96},{96,128},{128,160},{160,192},{192,2... | collective-permute-start | bytes 73736 | tf_op jit(solution)/shard_map/while/body/eval_jaxpr/ppermute | solution.py:11
  312.4 13.6 %collective-permute-start.4 = (f32[16]{0:T(128)S(1)}, f32[16]{0:T(128)S(1)}, u32[]{:S(2)}, u32[]{:S(2)}) collective-permute-start(f32[16]{0:T(128)S(1)} %copy.45), channel_id=1, source_target_pairs={{480,0},{0,32},{32,64},{64,96},{96,128},{128,160},{160,192},{192,2... | collective-permute-start | bytes 200 | tf_op jit(solution)/shard_map/while/body/eval_jaxpr/ppermute | solution.py:11
  317.1 15.5 %collective-permute-start.8 = (f32[16,768]{1,0:T(8,128)S(1)}, f32[16,768]{1,0:T(8,128)S(1)}, u32[]{:S(2)}, u32[]{:S(2)}) collective-permute-start(f32[16,768]{1,0:T(8,128)S(1)} %convolution_add_fusion.3), channel_id=1, source_target_pairs={{480,0},{0,32},{32,64},{64,96},{96,128},{128,160},{160,192},{192,2... | collective-permute-start | bytes 147464 | tf_op jit(solution)/shard_map/while/body/eval_jaxpr/ppermute | solution.py:11
  332.6 18.7 %collective-permute-start.6 = (f32[16]{0:T(128)S(1)}, f32[16]{0:T(128)S(1)}, u32[]{:S(2)}, u32[]{:S(2)}) collective-permute-start(f32[16]{0:T(128)S(1)} %copy.47), channel_id=1, source_target_pairs={{480,0},{0,32},{32,64},{64,96},{96,128},{128,160},{160,192},{192,2... | collective-permute-start | bytes 200 | tf_op jit(solution)/shard_map/while/body/eval_jaxpr/ppermute | solution.py:11
  334.5 23.3 %collective-permute-start.3 = (bf16[16,768]{1,0:T(8,128)(2,1)S(1)}, bf16[16,768]{1,0:T(8,128)(2,1)S(1)}, u32[]{:S(2)}, u32[]{:S(2)}) collective-permute-start(bf16[16,768]{1,0:T(8,128)(2,1)S(1)} %copy.44), channel_id=1, source_target_pairs={{480,0},{0,32},{32,64},{64,96},{96,128},{128,160},{160,192},{192,2... | collective-permute-start | bytes 73736 | tf_op jit(solution)/shard_map/while/body/eval_jaxpr/ppermute | solution.py:11
  337.6 13.6 %collective-permute-start.4 = (f32[16]{0:T(128)S(1)}, f32[16]{0:T(128)S(1)}, u32[]{:S(2)}, u32[]{:S(2)}) collective-permute-start(f32[16]{0:T(128)S(1)} %copy.45), channel_id=1, source_target_pairs={{480,0},{0,32},{32,64},{64,96},{96,128},{128,160},{160,192},{192,2... | collective-permute-start | bytes 200 | tf_op jit(solution)/shard_map/while/body/eval_jaxpr/ppermute | solution.py:11
  342.3 15.5 %collective-permute-start.8 = (f32[16,768]{1,0:T(8,128)S(1)}, f32[16,768]{1,0:T(8,128)S(1)}, u32[]{:S(2)}, u32[]{:S(2)}) collective-permute-start(f32[16,768]{1,0:T(8,128)S(1)} %convolution_add_fusion.3), channel_id=1, source_target_pairs={{480,0},{0,32},{32,64},{64,96},{96,128},{128,160},{160,192},{192,2... | collective-permute-start | bytes 147464 | tf_op jit(solution)/shard_map/while/body/eval_jaxpr/ppermute | solution.py:11
  357.9 18.7 %collective-permute-start.6 = (f32[16]{0:T(128)S(1)}, f32[16]{0:T(128)S(1)}, u32[]{:S(2)}, u32[]{:S(2)}) collective-permute-start(f32[16]{0:T(128)S(1)} %copy.47), channel_id=1, source_target_pairs={{480,0},{0,32},{32,64},{64,96},{96,128},{128,160},{160,192},{192,2... | collective-permute-start | bytes 200 | tf_op jit(solution)/shard_map/while/body/eval_jaxpr/ppermute | solution.py:11
  359.8 23.3 %collective-permute-start.3 = (bf16[16,768]{1,0:T(8,128)(2,1)S(1)}, bf16[16,768]{1,0:T(8,128)(2,1)S(1)}, u32[]{:S(2)}, u32[]{:S(2)}) collective-permute-start(bf16[16,768]{1,0:T(8,128)(2,1)S(1)} %copy.44), channel_id=1, source_target_pairs={{480,0},{0,32},{32,64},{64,96},{96,128},{128,160},{160,192},{192,2... | collective-permute-start | bytes 73736 | tf_op jit(solution)/shard_map/while/body/eval_jaxpr/ppermute | solution.py:11
  367.6 15.5 %collective-permute-start.8 = (f32[16,768]{1,0:T(8,128)S(1)}, f32[16,768]{1,0:T(8,128)S(1)}, u32[]{:S(2)}, u32[]{:S(2)}) collective-permute-start(f32[16,768]{1,0:T(8,128)S(1)} %convolution_add_fusion.3), channel_id=1, source_target_pairs={{480,0},{0,32},{32,64},{64,96},{96,128},{128,160},{160,192},{192,2... | collective-permute-start | bytes 147464 | tf_op jit(solution)/shard_map/while/body/eval_jaxpr/ppermute | solution.py:11
  383.1 18.7 %collective-permute-start.6 = (f32[16]{0:T(128)S(1)}, f32[16]{0:T(128)S(1)}, u32[]{:S(2)}, u32[]{:S(2)}) collective-permute-start(f32[16]{0:T(128)S(1)} %copy.47), channel_id=1, source_target_pairs={{480,0},{0,32},{32,64},{64,96},{96,128},{128,160},{160,192},{192,2... | collective-permute-start | bytes 200 | tf_op jit(solution)/shard_map/while/body/eval_jaxpr/ppermute | solution.py:11
  385.1 23.3 %collective-permute-start.3 = (bf16[16,768]{1,0:T(8,128)(2,1)S(1)}, bf16[16,768]{1,0:T(8,128)(2,1)S(1)}, u32[]{:S(2)}, u32[]{:S(2)}) collective-permute-start(bf16[16,768]{1,0:T(8,128)(2,1)S(1)} %copy.44), channel_id=1, source_target_pairs={{480,0},{0,32},{32,64},{64,96},{96,128},{128,160},{160,192},{192,2... | collective-permute-start | bytes 73736 | tf_op jit(solution)/shard_map/while/body/eval_jaxpr/ppermute | solution.py:11
  388.2 13.6 %collective-permute-start.4 = (f32[16]{0:T(128)S(1)}, f32[16]{0:T(128)S(1)}, u32[]{:S(2)}, u32[]{:S(2)}) collective-permute-start(f32[16]{0:T(128)S(1)} %copy.45), channel_id=1, source_target_pairs={{480,0},{0,32},{32,64},{64,96},{96,128},{128,160},{160,192},{192,2... | collective-permute-start | bytes 200 | tf_op jit(solution)/shard_map/while/body/eval_jaxpr/ppermute | solution.py:11
  392.9 15.5 %collective-permute-start.8 = (f32[16,768]{1,0:T(8,128)S(1)}, f32[16,768]{1,0:T(8,128)S(1)}, u32[]{:S(2)}, u32[]{:S(2)}) collective-permute-start(f32[16,768]{1,0:T(8,128)S(1)} %convolution_add_fusion.3), channel_id=1, source_target_pairs={{480,0},{0,32},{32,64},{64,96},{96,128},{128,160},{160,192},{192,2... | collective-permute-start | bytes 147464 | tf_op jit(solution)/shard_map/while/body/eval_jaxpr/ppermute | solution.py:11
  408.4 18.7 %collective-permute-start.6 = (f32[16]{0:T(128)S(1)}, f32[16]{0:T(128)S(1)}, u32[]{:S(2)}, u32[]{:S(2)}) collective-permute-start(f32[16]{0:T(128)S(1)} %copy.47), channel_id=1, source_target_pairs={{480,0},{0,32},{32,64},{64,96},{96,128},{128,160},{160,192},{192,2... | collective-permute-start | bytes 200 | tf_op jit(solution)/shard_map/while/body/eval_jaxpr/ppermute | solution.py:11
  410.3 23.3 %collective-permute-start.3 = (bf16[16,768]{1,0:T(8,128)(2,1)S(1)}, bf16[16,768]{1,0:T(8,128)(2,1)S(1)}, u32[]{:S(2)}, u32[]{:S(2)}) collective-permute-start(bf16[16,768]{1,0:T(8,128)(2,1)S(1)} %copy.44), channel_id=1, source_target_pairs={{480,0},{0,32},{32,64},{64,96},{96,128},{128,160},{160,192},{192,2... | collective-permute-start | bytes 73736 | tf_op jit(solution)/shard_map/while/body/eval_jaxpr/ppermute | solution.py:11
  413.5 13.6 %collective-permute-start.4 = (f32[16]{0:T(128)S(1)}, f32[16]{0:T(128)S(1)}, u32[]{:S(2)}, u32[]{:S(2)}) collective-permute-start(f32[16]{0:T(128)S(1)} %copy.45), channel_id=1, source_target_pairs={{480,0},{0,32},{32,64},{64,96},{96,128},{128,160},{160,192},{192,2... | collective-permute-start | bytes 200 | tf_op jit(solution)/shard_map/while/body/eval_jaxpr/ppermute | solution.py:11
  418.1 15.5 %collective-permute-start.8 = (f32[16,768]{1,0:T(8,128)S(1)}, f32[16,768]{1,0:T(8,128)S(1)}, u32[]{:S(2)}, u32[]{:S(2)}) collective-permute-start(f32[16,768]{1,0:T(8,128)S(1)} %convolution_add_fusion.3), channel_id=1, source_target_pairs={{480,0},{0,32},{32,64},{64,96},{96,128},{128,160},{160,192},{192,2... | collective-permute-start | bytes 147464 | tf_op jit(solution)/shard_map/while/body/eval_jaxpr/ppermute | solution.py:11
  433.7 18.7 %collective-permute-start.6 = (f32[16]{0:T(128)S(1)}, f32[16]{0:T(128)S(1)}, u32[]{:S(2)}, u32[]{:S(2)}) collective-permute-start(f32[16]{0:T(128)S(1)} %copy.47), channel_id=1, source_target_pairs={{480,0},{0,32},{32,64},{64,96},{96,128},{128,160},{160,192},{192,2... | collective-permute-start | bytes 200 | tf_op jit(solution)/shard_map/while/body/eval_jaxpr/ppermute | solution.py:11
  435.6 23.3 %collective-permute-start.3 = (bf16[16,768]{1,0:T(8,128)(2,1)S(1)}, bf16[16,768]{1,0:T(8,128)(2,1)S(1)}, u32[]{:S(2)}, u32[]{:S(2)}) collective-permute-start(bf16[16,768]{1,0:T(8,128)(2,1)S(1)} %copy.44), channel_id=1, source_target_pairs={{480,0},{0,32},{32,64},{64,96},{96,128},{128,160},{160,192},{192,2... | collective-permute-start | bytes 73736 | tf_op jit(solution)/shard_map/while/body/eval_jaxpr/ppermute | solution.py:11
  438.7 13.6 %collective-permute-start.4 = (f32[16]{0:T(128)S(1)}, f32[16]{0:T(128)S(1)}, u32[]{:S(2)}, u32[]{:S(2)}) collective-permute-start(f32[16]{0:T(128)S(1)} %copy.45), channel_id=1, source_target_pairs={{480,0},{0,32},{32,64},{64,96},{96,128},{128,160},{160,192},{192,2... | collective-permute-start | bytes 200 | tf_op jit(solution)/shard_map/while/body/eval_jaxpr/ppermute | solution.py:11
  443.4 15.5 %collective-permute-start.8 = (f32[16,768]{1,0:T(8,128)S(1)}, f32[16,768]{1,0:T(8,128)S(1)}, u32[]{:S(2)}, u32[]{:S(2)}) collective-permute-start(f32[16,768]{1,0:T(8,128)S(1)} %convolution_add_fusion.3), channel_id=1, source_target_pairs={{480,0},{0,32},{32,64},{64,96},{96,128},{128,160},{160,192},{192,2... | collective-permute-start | bytes 147464 | tf_op jit(solution)/shard_map/while/body/eval_jaxpr/ppermute | solution.py:11
  458.9 18.7 %collective-permute-start.6 = (f32[16]{0:T(128)S(1)}, f32[16]{0:T(128)S(1)}, u32[]{:S(2)}, u32[]{:S(2)}) collective-permute-start(f32[16]{0:T(128)S(1)} %copy.47), channel_id=1, source_target_pairs={{480,0},{0,32},{32,64},{64,96},{96,128},{128,160},{160,192},{192,2... | collective-permute-start | bytes 200 | tf_op jit(solution)/shard_map/while/body/eval_jaxpr/ppermute | solution.py:11
  460.9 23.3 %collective-permute-start.3 = (bf16[16,768]{1,0:T(8,128)(2,1)S(1)}, bf16[16,768]{1,0:T(8,128)(2,1)S(1)}, u32[]{:S(2)}, u32[]{:S(2)}) collective-permute-start(bf16[16,768]{1,0:T(8,128)(2,1)S(1)} %copy.44), channel_id=1, source_target_pairs={{480,0},{0,32},{32,64},{64,96},{96,128},{128,160},{160,192},{192,2... | collective-permute-start | bytes 73736 | tf_op jit(solution)/shard_map/while/body/eval_jaxpr/ppermute | solution.py:11
  468.7 15.5 %collective-permute-start.8 = (f32[16,768]{1,0:T(8,128)S(1)}, f32[16,768]{1,0:T(8,128)S(1)}, u32[]{:S(2)}, u32[]{:S(2)}) collective-permute-start(f32[16,768]{1,0:T(8,128)S(1)} %convolution_add_fusion.3), channel_id=1, source_target_pairs={{480,0},{0,32},{32,64},{64,96},{96,128},{128,160},{160,192},{192,2... | collective-permute-start | bytes 147464 | tf_op jit(solution)/shard_map/while/body/eval_jaxpr/ppermute | solution.py:11
  484.2 18.7 %collective-permute-start.6 = (f32[16]{0:T(128)S(1)}, f32[16]{0:T(128)S(1)}, u32[]{:S(2)}, u32[]{:S(2)}) collective-permute-start(f32[16]{0:T(128)S(1)} %copy.47), channel_id=1, source_target_pairs={{480,0},{0,32},{32,64},{64,96},{96,128},{128,160},{160,192},{192,2... | collective-permute-start | bytes 200 | tf_op jit(solution)/shard_map/while/body/eval_jaxpr/ppermute | solution.py:11
  486.1 23.3 %collective-permute-start.3 = (bf16[16,768]{1,0:T(8,128)(2,1)S(1)}, bf16[16,768]{1,0:T(8,128)(2,1)S(1)}, u32[]{:S(2)}, u32[]{:S(2)}) collective-permute-start(bf16[16,768]{1,0:T(8,128)(2,1)S(1)} %copy.44), channel_id=1, source_target_pairs={{480,0},{0,32},{32,64},{64,96},{96,128},{128,160},{160,192},{192,2... | collective-permute-start | bytes 73736 | tf_op jit(solution)/shard_map/while/body/eval_jaxpr/ppermute | solution.py:11
  489.3 13.6 %collective-permute-start.4 = (f32[16]{0:T(128)S(1)}, f32[16]{0:T(128)S(1)}, u32[]{:S(2)}, u32[]{:S(2)}) collective-permute-start(f32[16]{0:T(128)S(1)} %copy.45), channel_id=1, source_target_pairs={{480,0},{0,32},{32,64},{64,96},{96,128},{128,160},{160,192},{192,2... | collective-permute-start | bytes 200 | tf_op jit(solution)/shard_map/while/body/eval_jaxpr/ppermute | solution.py:11
  493.9 15.5 %collective-permute-start.8 = (f32[16,768]{1,0:T(8,128)S(1)}, f32[16,768]{1,0:T(8,128)S(1)}, u32[]{:S(2)}, u32[]{:S(2)}) collective-permute-start(f32[16,768]{1,0:T(8,128)S(1)} %convolution_add_fusion.3), channel_id=1, source_target_pairs={{480,0},{0,32},{32,64},{64,96},{96,128},{128,160},{160,192},{192,2... | collective-permute-start | bytes 147464 | tf_op jit(solution)/shard_map/while/body/eval_jaxpr/ppermute | solution.py:11
  509.5 18.7 %collective-permute-start.6 = (f32[16]{0:T(128)S(1)}, f32[16]{0:T(128)S(1)}, u32[]{:S(2)}, u32[]{:S(2)}) collective-permute-start(f32[16]{0:T(128)S(1)} %copy.47), channel_id=1, source_target_pairs={{480,0},{0,32},{32,64},{64,96},{96,128},{128,160},{160,192},{192,2... | collective-permute-start | bytes 200 | tf_op jit(solution)/shard_map/while/body/eval_jaxpr/ppermute | solution.py:11
  511.4 23.3 %collective-permute-start.3 = (bf16[16,768]{1,0:T(8,128)(2,1)S(1)}, bf16[16,768]{1,0:T(8,128)(2,1)S(1)}, u32[]{:S(2)}, u32[]{:S(2)}) collective-permute-start(bf16[16,768]{1,0:T(8,128)(2,1)S(1)} %copy.44), channel_id=1, source_target_pairs={{480,0},{0,32},{32,64},{64,96},{96,128},{128,160},{160,192},{192,2... | collective-permute-start | bytes 73736 | tf_op jit(solution)/shard_map/while/body/eval_jaxpr/ppermute | solution.py:11
  514.5 13.6 %collective-permute-start.4 = (f32[16]{0:T(128)S(1)}, f32[16]{0:T(128)S(1)}, u32[]{:S(2)}, u32[]{:S(2)}) collective-permute-start(f32[16]{0:T(128)S(1)} %copy.45), channel_id=1, source_target_pairs={{480,0},{0,32},{32,64},{64,96},{96,128},{128,160},{160,192},{192,2... | collective-permute-start | bytes 200 | tf_op jit(solution)/shard_map/while/body/eval_jaxpr/ppermute | solution.py:11
  519.2 15.5 %collective-permute-start.8 = (f32[16,768]{1,0:T(8,128)S(1)}, f32[16,768]{1,0:T(8,128)S(1)}, u32[]{:S(2)}, u32[]{:S(2)}) collective-permute-start(f32[16,768]{1,0:T(8,128)S(1)} %convolution_add_fusion.3), channel_id=1, source_target_pairs={{480,0},{0,32},{32,64},{64,96},{96,128},{128,160},{160,192},{192,2... | collective-permute-start | bytes 147464 | tf_op jit(solution)/shard_map/while/body/eval_jaxpr/ppermute | solution.py:11
  534.7 18.7 %collective-permute-start.6 = (f32[16]{0:T(128)S(1)}, f32[16]{0:T(128)S(1)}, u32[]{:S(2)}, u32[]{:S(2)}) collective-permute-start(f32[16]{0:T(128)S(1)} %copy.47), channel_id=1, source_target_pairs={{480,0},{0,32},{32,64},{64,96},{96,128},{128,160},{160,192},{192,2... | collective-permute-start | bytes 200 | tf_op jit(solution)/shard_map/while/body/eval_jaxpr/ppermute | solution.py:11
  536.7 23.3 %collective-permute-start.3 = (bf16[16,768]{1,0:T(8,128)(2,1)S(1)}, bf16[16,768]{1,0:T(8,128)(2,1)S(1)}, u32[]{:S(2)}, u32[]{:S(2)}) collective-permute-start(bf16[16,768]{1,0:T(8,128)(2,1)S(1)} %copy.44), channel_id=1, source_target_pairs={{480,0},{0,32},{32,64},{64,96},{96,128},{128,160},{160,192},{192,2... | collective-permute-start | bytes 73736 | tf_op jit(solution)/shard_map/while/body/eval_jaxpr/ppermute | solution.py:11
  539.8 13.6 %collective-permute-start.4 = (f32[16]{0:T(128)S(1)}, f32[16]{0:T(128)S(1)}, u32[]{:S(2)}, u32[]{:S(2)}) collective-permute-start(f32[16]{0:T(128)S(1)} %copy.45), channel_id=1, source_target_pairs={{480,0},{0,32},{32,64},{64,96},{96,128},{128,160},{160,192},{192,2... | collective-permute-start | bytes 200 | tf_op jit(solution)/shard_map/while/body/eval_jaxpr/ppermute | solution.py:11
  544.5 15.5 %collective-permute-start.8 = (f32[16,768]{1,0:T(8,128)S(1)}, f32[16,768]{1,0:T(8,128)S(1)}, u32[]{:S(2)}, u32[]{:S(2)}) collective-permute-start(f32[16,768]{1,0:T(8,128)S(1)} %convolution_add_fusion.3), channel_id=1, source_target_pairs={{480,0},{0,32},{32,64},{64,96},{96,128},{128,160},{160,192},{192,2... | collective-permute-start | bytes 147464 | tf_op jit(solution)/shard_map/while/body/eval_jaxpr/ppermute | solution.py:11
  560.0 18.7 %collective-permute-start.6 = (f32[16]{0:T(128)S(1)}, f32[16]{0:T(128)S(1)}, u32[]{:S(2)}, u32[]{:S(2)}) collective-permute-start(f32[16]{0:T(128)S(1)} %copy.47), channel_id=1, source_target_pairs={{480,0},{0,32},{32,64},{64,96},{96,128},{128,160},{160,192},{192,2... | collective-permute-start | bytes 200 | tf_op jit(solution)/shard_map/while/body/eval_jaxpr/ppermute | solution.py:11
  561.9 23.3 %collective-permute-start.3 = (bf16[16,768]{1,0:T(8,128)(2,1)S(1)}, bf16[16,768]{1,0:T(8,128)(2,1)S(1)}, u32[]{:S(2)}, u32[]{:S(2)}) collective-permute-start(bf16[16,768]{1,0:T(8,128)(2,1)S(1)} %copy.44), channel_id=1, source_target_pairs={{480,0},{0,32},{32,64},{64,96},{96,128},{128,160},{160,192},{192,2... | collective-permute-start | bytes 73736 | tf_op jit(solution)/shard_map/while/body/eval_jaxpr/ppermute | solution.py:11
  565.1 13.6 %collective-permute-start.4 = (f32[16]{0:T(128)S(1)}, f32[16]{0:T(128)S(1)}, u32[]{:S(2)}, u32[]{:S(2)}) collective-permute-start(f32[16]{0:T(128)S(1)} %copy.45), channel_id=1, source_target_pairs={{480,0},{0,32},{32,64},{64,96},{96,128},{128,160},{160,192},{192,2... | collective-permute-start | bytes 200 | tf_op jit(solution)/shard_map/while/body/eval_jaxpr/ppermute | solution.py:11
  569.8 15.5 %collective-permute-start.8 = (f32[16,768]{1,0:T(8,128)S(1)}, f32[16,768]{1,0:T(8,128)S(1)}, u32[]{:S(2)}, u32[]{:S(2)}) collective-permute-start(f32[16,768]{1,0:T(8,128)S(1)} %convolution_add_fusion.3), channel_id=1, source_target_pairs={{480,0},{0,32},{32,64},{64,96},{96,128},{128,160},{160,192},{192,2... | collective-permute-start | bytes 147464 | tf_op jit(solution)/shard_map/while/body/eval_jaxpr/ppermute | solution.py:11
  585.3 18.7 %collective-permute-start.6 = (f32[16]{0:T(128)S(1)}, f32[16]{0:T(128)S(1)}, u32[]{:S(2)}, u32[]{:S(2)}) collective-permute-start(f32[16]{0:T(128)S(1)} %copy.47), channel_id=1, source_target_pairs={{480,0},{0,32},{32,64},{64,96},{96,128},{128,160},{160,192},{192,2... | collective-permute-start | bytes 200 | tf_op jit(solution)/shard_map/while/body/eval_jaxpr/ppermute | solution.py:11
  587.2 23.3 %collective-permute-start.3 = (bf16[16,768]{1,0:T(8,128)(2,1)S(1)}, bf16[16,768]{1,0:T(8,128)(2,1)S(1)}, u32[]{:S(2)}, u32[]{:S(2)}) collective-permute-start(bf16[16,768]{1,0:T(8,128)(2,1)S(1)} %copy.44), channel_id=1, source_target_pairs={{480,0},{0,32},{32,64},{64,96},{96,128},{128,160},{160,192},{192,2... | collective-permute-start | bytes 73736 | tf_op jit(solution)/shard_map/while/body/eval_jaxpr/ppermute | solution.py:11
  590.3 13.6 %collective-permute-start.4 = (f32[16]{0:T(128)S(1)}, f32[16]{0:T(128)S(1)}, u32[]{:S(2)}, u32[]{:S(2)}) collective-permute-start(f32[16]{0:T(128)S(1)} %copy.45), channel_id=1, source_target_pairs={{480,0},{0,32},{32,64},{64,96},{96,128},{128,160},{160,192},{192,2... | collective-permute-start | bytes 200 | tf_op jit(solution)/shard_map/while/body/eval_jaxpr/ppermute | solution.py:11
  595.0 15.5 %collective-permute-start.8 = (f32[16,768]{1,0:T(8,128)S(1)}, f32[16,768]{1,0:T(8,128)S(1)}, u32[]{:S(2)}, u32[]{:S(2)}) collective-permute-start(f32[16,768]{1,0:T(8,128)S(1)} %convolution_add_fusion.3), channel_id=1, source_target_pairs={{480,0},{0,32},{32,64},{64,96},{96,128},{128,160},{160,192},{192,2... | collective-permute-start | bytes 147464 | tf_op jit(solution)/shard_map/while/body/eval_jaxpr/ppermute | solution.py:11
  610.5 18.7 %collective-permute-start.6 = (f32[16]{0:T(128)S(1)}, f32[16]{0:T(128)S(1)}, u32[]{:S(2)}, u32[]{:S(2)}) collective-permute-start(f32[16]{0:T(128)S(1)} %copy.47), channel_id=1, source_target_pairs={{480,0},{0,32},{32,64},{64,96},{96,128},{128,160},{160,192},{192,2... | collective-permute-start | bytes 200 | tf_op jit(solution)/shard_map/while/body/eval_jaxpr/ppermute | solution.py:11
  612.5 23.3 %collective-permute-start.3 = (bf16[16,768]{1,0:T(8,128)(2,1)S(1)}, bf16[16,768]{1,0:T(8,128)(2,1)S(1)}, u32[]{:S(2)}, u32[]{:S(2)}) collective-permute-start(bf16[16,768]{1,0:T(8,128)(2,1)S(1)} %copy.44), channel_id=1, source_target_pairs={{480,0},{0,32},{32,64},{64,96},{96,128},{128,160},{160,192},{192,2... | collective-permute-start | bytes 73736 | tf_op jit(solution)/shard_map/while/body/eval_jaxpr/ppermute | solution.py:11
  620.3 15.5 %collective-permute-start.8 = (f32[16,768]{1,0:T(8,128)S(1)}, f32[16,768]{1,0:T(8,128)S(1)}, u32[]{:S(2)}, u32[]{:S(2)}) collective-permute-start(f32[16,768]{1,0:T(8,128)S(1)} %convolution_add_fusion.3), channel_id=1, source_target_pairs={{480,0},{0,32},{32,64},{64,96},{96,128},{128,160},{160,192},{192,2... | collective-permute-start | bytes 147464 | tf_op jit(solution)/shard_map/while/body/eval_jaxpr/ppermute | solution.py:11
  654.9 415.0 %all-reduce.5.cloned.1.call-start = ((), (), s32[]{:S(2)}) async-start(), calls=%async_computation.1 | async-start | bytes 1572864 | tf_op jit(solution)/shard_map/psum | solution.py:161
  (88 other events, 723.9 us)
Sparse Core Ops, SparseCore 0:
  655.1 241.4 all-reduce.2
  899.4 170.4 all-reduce.4
